TPU v7x, 256 devices: a whole 4x4x8 slice. The times are simulated.
256 devices in a mesh: section: 8 (over z), dp: 32 (over x, y, core).
Axes of the slice: x: 4, y: 4, z: 8, core: 2. Of those that a mesh axis runs over, the one named last changes fastest.
Arguments:
- output_gradient: bfloat16 [8, 4096, 2048], P('section', 'dp'), may hold values from -6 to 6
- saved_input: bfloat16 [8, 4096, 8192], P('section', 'dp'), may hold values from -6 to 6
- frozen_matrix: bfloat16 [8, 8192, 2048], P('section', 'dp'), may hold values from -0.0625 to 0.0625
- adapter_down_maps: bfloat16 [8, 8192, 2048], P('section', None, 'dp'), may hold values from -0.0625 to 0.0625
- adapter_up_maps: bfloat16 [8, 2048, 2048], P('section', None, 'dp'), may hold values from -0.125 to 0.125
- token_tenants: int32 [8, 4096], P('section'), may hold values from 0 to 31, never falling along the last dimension, each value on 1 to 256 neighbouring positions
- tenant_slot_lookup: int32 [8, 32], P('section'), may hold values from 0 to 31, each once within a row
Outputs:
- passed_grad: bfloat16 [8, 4096, 8192], P('section', 'dp')
- down_gradient: bfloat16 [8, 8192, 2048], P('section', None, 'dp')
- up_gradient: bfloat16 [8, 2048, 2048], P('section', None, 'dp')
Inputs may be any that keep to these rules, and one draw needn't show every extreme that they name: `token_tenants`: within a section the ids never fall; each of the 32 tenants has 1 to 256 tokens, one exactly 256. `tenant_slot_lookup`: each section's row is a permutation.
All inputs are finite; a program needn't handle non-finite values.
Results may differ from a plain program's by a relative error of at most 0.005.
Values may be sent and summed in bfloat16 or wider, within the bound.
A program may use at most 128 MiB of HBM per device.

v0:
```python
import jax
import jax.numpy as jnp
from jax import lax
from jax.sharding import PartitionSpec as P

ADAPTER_RANK = 64
MOST = 256


adapter_scale = 2.0


def from_behind(value, axis, steps):
    count = lax.axis_size(axis)
    first, last = (max(0, -steps), min(count, count - steps))
    return lax.ppermute(value, axis, [(source, source + steps) for source in range(first, last)])


def block_layout(tenant_row, slot_table, tenants, most):
    tokens = tenant_row.shape[0]
    tenant_range = jnp.arange(tenants, dtype=jnp.int32)
    member = (tenant_range[:, None] == tenant_row[None, :]).astype(jnp.int32)
    counts = jnp.sum(member, axis=1)
    starts = jnp.cumsum(counts) - counts
    owner_match = (slot_table[None, :] == tenant_range[:, None]).astype(jnp.int32)
    slot_start = jnp.sum(owner_match * starts[None, :], axis=1)
    slot_count = jnp.sum(owner_match * counts[None, :], axis=1)
    place = jnp.arange(most, dtype=jnp.int32)
    live_slot = place[None, :] < slot_count[:, None]
    row_index = jnp.minimum(slot_start[:, None] + place[None, :], tokens - 1)
    token_slot = jnp.sum(member * slot_table[:, None], axis=0)
    token_start = jnp.sum(member * starts[:, None], axis=0)
    token_place = token_slot * most + jnp.arange(tokens, dtype=jnp.int32) - token_start
    return (row_index, live_slot, token_place)


def masked_rows(rows, row_index, live_slot):
    picked = rows[row_index]
    return jnp.where(live_slot[:, :, None], picked, jnp.zeros((), picked.dtype))


def adapter_term(rank_up_values, down_three, token_place):
    blocks = jnp.einsum(
        "kpr,dkr->kpd", rank_up_values, down_three, preferred_element_type=jnp.float32
    )
    return blocks.reshape(blocks.shape[0] * blocks.shape[1], blocks.shape[2])[token_place]


def local(
    output_gradient,
    saved_input,
    frozen_matrix,
    adapter_down_maps,
    adapter_up_maps,
    token_tenants,
    tenant_slot_lookup,
):
    grad_rows = output_gradient[0]
    saved_rows = saved_input[0]
    weight = frozen_matrix[0]
    local_width = weight.shape[0]
    out_width = weight.shape[1]
    kv_local = out_width // lax.axis_size("dp")
    kv_offset = lax.axis_index("dp") * kv_local
    tenants = tenant_slot_lookup.shape[1]
    contract_last = (((1,), (1,)), ((), ()))
    row_index, live_slot, token_place = block_layout(
        token_tenants[0], tenant_slot_lookup[0], tenants, MOST
    )
    saved_cols = lax.all_to_all(saved_rows, "dp", split_axis=1, concat_axis=0, tiled=True)
    saved_input_blocks = masked_rows(saved_cols, row_index, live_slot)
    block_rows = lax.all_gather(grad_rows, "dp", axis=0, tiled=True)
    frozen_part = lax.dot_general(
        block_rows, weight, contract_last, preferred_element_type=jnp.float32
    )
    own_cols = lax.dynamic_slice_in_dim(block_rows, kv_offset, kv_local, 1).astype(jnp.float32)
    joined = jnp.concatenate([frozen_part, own_cols], axis=1)
    frozen_product = joined[:, :local_width]
    grad_cols = joined[:, local_width:].astype(jnp.bfloat16)
    down_cols, up_cols = (
        lax.all_to_all(adapter_down_maps[0], "dp", split_axis=0, concat_axis=1, tiled=True),
        lax.all_to_all(adapter_up_maps[0], "dp", split_axis=0, concat_axis=1, tiled=True),
    )
    down_three = down_cols.reshape(local_width, tenants, ADAPTER_RANK)
    up_three = up_cols.reshape(kv_local, tenants, ADAPTER_RANK)
    gradient_blocks = masked_rows(grad_cols, row_index, live_slot)
    up_part = jnp.einsum(
        "kpe,ekr->kpr", gradient_blocks, up_three, preferred_element_type=jnp.float32
    )
    down_part = jnp.einsum(
        "kpd,dkr->kpr", saved_input_blocks, down_three, preferred_element_type=jnp.float32
    )
    up_total, down_total = lax.psum((up_part, down_part), "dp")
    rank_up_values = up_total.astype(jnp.bfloat16)
    rank_down_values = down_total.astype(jnp.bfloat16)
    adapter_slot = adapter_term(rank_up_values, down_three, token_place)
    down_grad_cols = (
        (
            adapter_scale
            * jnp.einsum(
                "tfv,tfy->vty",
                saved_input_blocks,
                rank_up_values,
                preferred_element_type=jnp.float32,
            )
        )
        .reshape(local_width, tenants * ADAPTER_RANK)
        .astype(jnp.bfloat16)
    )
    up_grad_cols = (
        (
            adapter_scale
            * jnp.einsum(
                "ohz,ohq->zoq",
                gradient_blocks,
                rank_down_values,
                preferred_element_type=jnp.float32,
            )
        )
        .reshape(kv_local, tenants * ADAPTER_RANK)
        .astype(jnp.bfloat16)
    )
    down_gradient, up_gradient = (
        lax.all_to_all(down_grad_cols, "dp", split_axis=1, concat_axis=0, tiled=True),
        lax.all_to_all(up_grad_cols, "dp", split_axis=1, concat_axis=0, tiled=True),
    )
    input_columns = (frozen_product + adapter_scale * adapter_slot).astype(jnp.bfloat16)
    input_rows = lax.all_to_all(input_columns, "dp", split_axis=0, concat_axis=1, tiled=True)
    passed = from_behind(input_rows, "section", -1)
    return (passed[None], down_gradient[None], up_gradient[None])


def solution(mesh):
    return jax.shard_map(
        local,
        mesh=mesh,
        in_specs=(
            P("section", "dp", None),
            P("section", "dp", None),
            P("section", "dp", None),
            P("section", None, "dp"),
            P("section", None, "dp"),
            P("section", None),
            P("section", None),
        ),
        out_specs=(P("section", "dp", None), P("section", None, "dp"), P("section", None, "dp")),
        check_vma=False,
    )
```

profile of v0, /device:TPU:1, one launch (start us, length us, event | category | flops | bytes accessed | tf_op | source)
XLA Modules:
  0.0 439.3 jit_solution(11001682472240546703)
XLA Ops:
  7.9 2.3 all_to_all.72
  10.2 2.0 copy.35
  12.2 2.1 reshape.196
  14.4 8.6 %all-to-all-start = ((bf16[32,2,2048]{2,1,0:T(2,128)(2,1)}), bf16[32,2,2048]{2,1,0:T(2,128)(2,1)S(1)}, u32[]{:S(2)}, u32[]{:S(2)}) async-start(bf16[32,2,2048]{2,1,0:T(2,128)(2,1)} %reshape.196), calls=%async_computation | async-start | bytes 524288 | tf_op jit(solution)/shard_map/all_to_all | solution.py:82
  23.6 2.5 copy.27
  26.1 6.0 %all-to-all-done = bf16[32,2,2048]{2,1,0:T(2,128)(2,1)S(1)} async-done(((bf16[32,2,2048]{2,1,0:T(2,128)(2,1)}), bf16[32,2,2048]{2,1,0:T(2,128)(2,1)S(1)}, u32[]{:S(2)}, u32[]{:S(2)}) %all-to-all-start) | async-done | bytes 262176 | tf_op jit(solution)/shard_map/all_to_all | solution.py:82
  32.1 3.8 all-to-all-start.3
  36.6 1.5 copy.32
  38.1 1.6 copy.25
  39.9 25.3 %all-to-all-done.3 = bf16[128,32,256]{2,0,1:T(8,128)(2,1)S(1)} async-done(((bf16[128,32,256]{2,0,1:T(8,128)(2,1)}), bf16[128,32,256]{2,0,1:T(8,128)(2,1)S(1)}, u32[]{:S(2)}, u32[]{:S(2)}) %all-to-all-start.3) | async-done | bytes 2097184 | tf_op jit(solution)/shard_map/all_to_all | solution.py:70
  65.2 5.5 %all-to-all-start.1 = ((bf16[32,256,64]{1,2,0:T(8,128)(2,1)}), bf16[32,256,64]{1,2,0:T(8,128)(2,1)}, u32[]{:S(2)}, u32[]{:S(2)}) async-start(bf16[32,256,64]{1,2,0:T(8,128)(2,1)} %copy.25), calls=%async_computation.1 | async-start | bytes 2097152 | tf_op jit(solution)/shard_map/all_to_all | solution.py:81
  72.0 33.1 %gather_fusion.2 = bf16[8192,256]{1,0:T(8,128)(2,1)} fusion(bf16[4096,256]{1,0:T(8,128)(2,1)S(1)} %bitcast.79, s32[8192]{0:T(1024)S(1)} %broadcast_clamp_fusion), kind=kCustom, calls=%fused_computation.2 | custom fusion | bytes 8421376 | tf_op jit(solution)/shard_map/gather | solution.py:38
  105.1 4.6 %fusion.8 = f32[32,256,64]{1,2,0:T(8,128)} fusion(bf16[32,256,256]{2,1,0:T(8,128)(2,1)} %bitcast.86, pred[32,256]{1,0:T(8,128)(4,1)S(1)} %iota_compare_fusion.1, bf16[32,256,64]{1,2,0:T(8,128)(2,1)} %all-to-all-done.1), kind=kOutput, calls=%fused_computation.8 | convolution fusion | flops 270532608 | bytes 7348224 | tf_op jit(solution)/shard_map/kpd,dkr->kpr/dot_general | solution.py:90
  109.7 12.3 %all-gather.3.cloned.1.call-done = bf16[1,4096,2048]{2,1,0:T(8,128)(2,1)} async-done(((bf16[1,128,2048]{2,1,0:T(8,128)(2,1)}), bf16[1,4096,2048]{2,1,0:T(8,128)(2,1)}) %all-gather.3.cloned.1.call-update) | async-done | bytes 16777232 | tf_op jit(solution)/shard_map/all_gather | solution.py:72
  122.0 1.6 dynamic-slice_bitcast_fusion
  123.5 29.5 %gather_fusion = bf16[8192,64]{1,0:T(8,128)(2,1)} fusion(bf16[4096,64]{1,0:T(8,128)(2,1)S(1)} %dynamic-slice_bitcast_fusion, s32[8192]{0:T(1024)S(1)} %broadcast_clamp_fusion), kind=kCustom, calls=%fused_computation | custom fusion | bytes 2129920 | tf_op jit(solution)/shard_map/gather | solution.py:38
  153.0 2.7 copy.23
  155.7 1.8 fusion.20
  157.5 146.1 %all-reduce.2 = (bf16[32,256,64]{1,2,0:T(8,128)(2,1)}, bf16[32,256,64]{1,2,0:T(8,128)(2,1)}) all-reduce(f32[32,256,64]{1,2,0:T(8,128)S(1)} %fusion.20, f32[32,256,64]{1,2,0:T(8,128)} %fusion.8), channel_id=1, replica_groups=mesh['section'=8,'dp'=32] {'dp'}, use_global_device_ids=true, to_apply=%region_4.5 | all-reduce | flops 1048576 | bytes 6291456 | tf_op jit(solution)/shard_map/psum | solution.py:93
  303.6 6.1 %fusion.16 = f32[32,256,256]{2,1,0:T(8,128)} fusion(bf16[32,256,64]{1,2,0:T(8,128)(2,1)} %all-to-all-done.1, bf16[32,256,64]{1,2,0:T(8,128)(2,1)} %get-tuple-element.7), kind=kOutput, calls=%fused_computation.18 | convolution fusion | flops 268435456 | bytes 10485760 | tf_op jit(solution)/shard_map/kpr,dkr->kpd/dot_general | solution.py:43
  309.7 19.5 %gather_fusion.1 = f32[4096,256]{1,0:T(8,128)} fusion(f32[8192,256]{1,0:T(8,128)} %bitcast.80, s32[4096]{0:T(1024)S(1)} %broadcast_clamp_fusion.1), kind=kCustom, calls=%fused_computation.1 | custom fusion | bytes 8404992 | tf_op jit(solution)/shard_map/gather | solution.py:46
  329.2 11.8 %fusion.5 = bf16[4096,256]{1,0:T(8,128)(2,1)S(1)} fusion(bf16[1,4096,2048]{2,1,0:T(8,128)(2,1)} %all-gather.3.cloned.1.call-done, f32[4096,256]{1,0:T(8,128)} %gather_fusion.1, bf16[1,256,2048]{2,1,0:T(8,128)(2,1)S(1)} %copy-done), kind=kOutput, calls=%fused_computation.6 | convolution fusion | flops 4298113024 | bytes 24117248 | tf_op jit(solution)/shard_map/dot_general | solution.py:73
  341.1 37.0 %all_to_all.96 = bf16[32,128,256]{2,1,0:T(8,128)(2,1)S(1)} all-to-all(bf16[32,128,256]{2,1,0:T(8,128)(2,1)S(1)} %bitcast.89), channel_id=1, replica_groups=mesh['section'=8,'dp'=32] {'dp'}, dimensions={0} | all-to-all | bytes 4194304 | tf_op jit(solution)/shard_map/all_to_all | solution.py:128
  378.1 1.5 copy.30
  382.5 3.9 all-to-all-start.5
  386.4 4.8 %fusion.12 = bf16[256,32,64]{0,2,1:T(8,128)(2,1)} fusion(bf16[32,256,256]{2,1,0:T(8,128)(2,1)} %bitcast.87, pred[32,256]{1,0:T(8,128)(4,1)S(1)} %iota_compare_fusion.1, bf16[32,256,64]{1,2,0:T(8,128)(2,1)S(1)} %copy-done.3), kind=kOutput, calls=%fused_computation.13 | convolution fusion | flops 271581184 | bytes 6299648 | tf_op jit(solution)/shard_map/tfv,tfy->vty/dot_general | solution.py:100
  391.2 4.2 all-to-all-done.5
  395.4 3.8 all-to-all-start.4
  401.1 15.1 %all-to-all-done.4 = bf16[256,32,64]{0,2,1:T(8,128)(2,1)S(1)} async-done(((bf16[256,32,64]{0,2,1:T(8,128)(2,1)}), bf16[256,32,64]{0,2,1:T(8,128)(2,1)S(1)}, u32[]{:S(2)}, u32[]{:S(2)}) %all-to-all-start.4) | async-done | bytes 1048608 | tf_op jit(solution)/shard_map/all_to_all | solution.py:124
  416.8 1.3 broadcast_in_dim.52
  418.1 11.3 %collective-permute-done = bf16[128,8192]{1,0:T(8,128)(2,1)} collective-permute-done((bf16[128,8192]{1,0:T(8,128)(2,1)}, bf16[128,8192]{1,0:T(8,128)(2,1)}, u32[]{:S(2)}, u32[]{:S(2)}) %collective-permute-start) | collective-permute-done | bytes 2097184 | tf_op jit(solution)/shard_map/ppermute | solution.py:16
  429.4 3.1 copy.41
  (41 shorter events, 8.8 us)
Async XLA Ops:
  7.2 322.1 %copy-start = (bf16[1,256,2048]{2,1,0:T(8,128)(2,1)S(1)}, bf16[1,256,2048]{2,1,0:T(8,128)(2,1)}, u32[]{:S(2)}) copy-start(bf16[1,256,2048]{2,1,0:T(8,128)(2,1)} %param.9) | copy-start | bytes 3145732
  7.2 15.8 %copy-start.2 = (bf16[1,128,8192]{2,1,0:T(8,128)(2,1)S(1)}, bf16[1,128,8192]{2,1,0:T(8,128)(2,1)}, u32[]{:S(2)}) copy-start(bf16[1,128,8192]{2,1,0:T(8,128)(2,1)} %param.8) | copy-start | bytes 6291460
  7.2 114.8 %all-gather.3.cloned.1.call-start = ((), (), s32[]{:S(2)}) async-start(), calls=%async_computation.6 | async-start | bytes 17301504 | tf_op jit(solution)/shard_map/all_gather | solution.py:72
  14.4 17.7 %all-to-all-start = ((bf16[32,2,2048]{2,1,0:T(2,128)(2,1)}), bf16[32,2,2048]{2,1,0:T(2,128)(2,1)S(1)}, u32[]{:S(2)}, u32[]{:S(2)}) async-start(bf16[32,2,2048]{2,1,0:T(2,128)(2,1)} %reshape.196), calls=%async_computation | async-start | bytes 524288 | tf_op jit(solution)/shard_map/all_to_all | solution.py:82
  23.6 12.3 %copy-start.4 = (s32[1,4096]{1,0:T(1,128)S(1)}, s32[1,4096]{1,0:T(1,128)}, u32[]{:S(2)}) copy-start(s32[1,4096]{1,0:T(1,128)} %param.12) | copy-start | bytes 49156
  23.6 12.7 %copy-start.5 = (s32[1,32]{1,0:T(1,128)S(1)}, s32[1,32]{1,0:T(1,128)}, u32[]{:S(2)}) copy-start(s32[1,32]{1,0:T(1,128)} %param.13) | copy-start | bytes 388
  32.1 33.2 %all-to-all-start.3 = ((bf16[128,32,256]{2,0,1:T(8,128)(2,1)}), bf16[128,32,256]{2,0,1:T(8,128)(2,1)S(1)}, u32[]{:S(2)}, u32[]{:S(2)}) async-start(bf16[128,32,256]{2,0,1:T(8,128)(2,1)} %copy.27), calls=%async_computation.3 | async-start | bytes 4194304 | tf_op jit(solution)/shard_map/all_to_all | solution.py:70
  65.2 39.9 %all-to-all-start.1 = ((bf16[32,256,64]{1,2,0:T(8,128)(2,1)}), bf16[32,256,64]{1,2,0:T(8,128)(2,1)}, u32[]{:S(2)}, u32[]{:S(2)}) async-start(bf16[32,256,64]{1,2,0:T(8,128)(2,1)} %copy.25), calls=%async_computation.1 | async-start | bytes 2097152 | tf_op jit(solution)/shard_map/all_to_all | solution.py:81
  341.0 39.9 %copy-start.1 = (bf16[32,256,64]{1,2,0:T(8,128)(2,1)S(1)}, bf16[32,256,64]{1,2,0:T(8,128)(2,1)}, u32[]{:S(2)}) copy-start(bf16[32,256,64]{1,2,0:T(8,128)(2,1)} %copy.23) | copy-start | bytes 3145732
  341.1 39.9 %copy-start.6 = (bf16[32,256,64]{1,2,0:T(8,128)(2,1)S(1)}, bf16[32,256,64]{1,2,0:T(8,128)(2,1)}, u32[]{:S(2)}) copy-start(bf16[32,256,64]{1,2,0:T(8,128)(2,1)} %get-tuple-element.8) | copy-start | bytes 3145732
  378.1 8.3 %copy-start.3 = (bf16[32,256,64]{1,2,0:T(8,128)(2,1)S(1)}, bf16[32,256,64]{1,2,0:T(8,128)(2,1)}, u32[]{:S(2)}) copy-start(bf16[32,256,64]{1,2,0:T(8,128)(2,1)} %get-tuple-element.7) | copy-start | bytes 3145732
  379.6 49.8 %collective-permute-start = (bf16[128,8192]{1,0:T(8,128)(2,1)}, bf16[128,8192]{1,0:T(8,128)(2,1)}, u32[]{:S(2)}, u32[]{:S(2)}) collective-permute-start(bf16[128,8192]{1,0:T(8,128)(2,1)} %bitcast.25), channel_id=1, source_target_pairs={{32,0},{64,32},{96,64},{128,96},{160,128},{192,160},{224,192},{33,... | collective-permute-start | bytes 6291464 | tf_op jit(solution)/shard_map/ppermute | solution.py:16
  382.5 12.9 %all-to-all-start.5 = ((bf16[32,2,2048]{2,1,0:T(2,128)(2,1)}), bf16[32,2,2048]{2,1,0:T(2,128)(2,1)S(1)}, u32[]{:S(2)}, u32[]{:S(2)}) async-start(bf16[32,2,2048]{2,1,0:T(2,128)(2,1)} %reshape.198), calls=%async_computation.5 | async-start | bytes 524288 | tf_op jit(solution)/shard_map/all_to_all | solution.py:125
  395.4 20.8 %all-to-all-start.4 = ((bf16[256,32,64]{0,2,1:T(8,128)(2,1)}), bf16[256,32,64]{0,2,1:T(8,128)(2,1)S(1)}, u32[]{:S(2)}, u32[]{:S(2)}) async-start(bf16[256,32,64]{0,2,1:T(8,128)(2,1)} %fusion.12), calls=%async_computation.4 | async-start | bytes 2097152 | tf_op jit(solution)/shard_map/all_to_all | solution.py:124
Sparse Core Ops, SparseCore 0:
  10.6 111.3 all-gather.2
where the time goes:
time: 440 us; the launch traced here: 439 us
  blocking collectives  183 us (42%)
  local copies, waits for them, and re-layouts  110 us (25%)
  waiting for transfers between devices  74.7 us (17%)
  matrix products  29.6 us (7%)
  starting transfers between devices  26.9 us (6%)
  between operations  14.3 us (3%)
    psum x1, blocking collectives, local(): up_total, down_total = lax.psum((up_part, down_part), 'dp')  146 us
    gather x3, local copies, waits for them, and re-layouts, masked_rows(): picked = rows[row_index]  65.3 us
    all_to_all x1, blocking collectives, local(): lax.all_to_all(input_columns, 'dp', split_axis=0, concat_axis=1, tiled=True)  37 us
    all_to_all x1, waiting for transfers between devices, local(): lax.all_to_all(saved_rows, 'dp', split_axis=1, concat_axis=0, tiled=True)  25.3 us
    gather x1, local copies, waits for them, and re-layouts, adapter_term(): blocks.reshape(blocks.shape[0] * blocks.shape[1], blocks.shape[2])  19.5 us
    all_to_all x1, waiting for transfers between devices, local(): lax.all_to_all(down_grad_cols, 'dp', split_axis=1, concat_axis=0, tiled=T...  15.1 us
    all_gather x1, waiting for transfers between devices, local(): block_rows = lax.all_gather(grad_rows, 'dp', axis=0, tiled=True)  12.3 us
    dot_general x1, matrix products, local(): lax.dot_general(block_rows, weight, contract_last, preferred_element_type...  11.8 us
  transfers between devices with their start and end apart: 7, of which 6 were waited for; matrix products, arithmetic and copies ran while one was open for 14% of the time, Pallas kernels for 0%

commit v1 on v0

v1 whole, which is shorter than its diff:
```python
import jax
import jax.numpy as jnp
from jax import lax
from jax.experimental import pallas as pl
from jax.experimental.pallas import tpu as pltpu
from jax.sharding import PartitionSpec as P

RANK = 64
WIN = 288
HALF = WIN // 2
PAD = 256
MESH = pl.DeviceIdType.MESH
NT = (((1,), (1,)), ((), ()))
NN = (((1,), (0,)), ((), ()))
TN = (((0,), (0,)), ((), ()))
F32 = jnp.float32
BF16 = jnp.bfloat16


def dot(a, b, dims):
    return lax.dot_general(a, b, dims, preferred_element_type=F32)


def remote(src, dst, send, recv, device):
    return pltpu.make_async_remote_copy(
        src_ref=src, dst_ref=dst, send_sem=send, recv_sem=recv, device_id=device, device_id_type=MESH
    )


def kernel(
    meta, spots, mask, g_hbm, x_hbm, w_ref, at_hbm, ut_ref, passed, da_out, du_out,
    g_all, xf, atf, upad, usib, uexp, p_stage, da_stage, vp, vsib, vrecv, vbf, dubuf, zero,
    loc, ag_s, ag_r, sb_s, sb_r, x_s, x_r, a_s, a_r, us_s, us_r, u_s, u_r, uf_s, uf_r,
    p_s, p_r, da_s, da_r, vs_s, vs_r, v_s, v_r, vb_s, vb_r,
):
    z = lax.axis_index("section")
    me = lax.axis_index("dp")
    last = lax.axis_size("section") - 1
    core = lax.rem(me, 2)
    other = 1 - core
    chip = me // 2
    x, y = chip // 4, lax.rem(chip, 4)
    sib = chip * 2 + other
    width = w_ref.shape[0]
    rows = g_hbm.shape[0]

    def at(dx, dy):
        return lax.rem(x + dx, 4) * 4 + lax.rem(y + dy, 4)

    def start_of(slot):
        return meta[slot] * 16

    def node(p, a, b, who=core):
        return (at(b % 4, a % 4) if p == 0 else at(a % 4, b % 4)) * 2 + who

    def chunk(device, p, part=None):
        first = device * rows + p * 64
        if part is None:
            return g_all.at[pl.ds(pl.multiple_of(first, 64), 64)]
        return g_all.at[pl.ds(pl.multiple_of(first + part * 32, 32), 32)]

    def ag(src, dst, slot, device):
        return remote(src, dst, ag_s.at[slot], ag_r.at[slot], {"dp": device})

    def part_of(d):
        return 0 if d == 1 else 1

    def first(p, d):
        return ag(g_hbm.at[pl.ds(p * 64, 64)], chunk(me, p), p * 20 + part_of(d), node(p, d, 0))

    def got_first(p, d):
        c = chunk(node(p, -d, 0), p)
        ag(c, c, p * 20 + part_of(d), me).wait_recv()

    def fwd1(p, d):
        c = chunk(node(p, -d, 0), p, part_of(d))
        return ag(c, c, p * 20 + 2 + part_of(d), node(p, d, 0))

    def got_fwd1(p, d):
        c = chunk(node(p, 2, 0), p, part_of(d))
        ag(c, c, p * 20 + 2 + part_of(d), me).wait_recv()

    def second(p, q, d):
        c = chunk(node(p, q, 0), p)
        src = g_hbm.at[pl.ds(p * 64, 64)] if q == 0 else c
        return ag(src, c, p * 20 + 4 + q * 4 + part_of(d), node(p, 0, d))

    def got_second(p, q, d):
        c = chunk(node(p, q, -d), p)
        ag(c, c, p * 20 + 4 + q * 4 + part_of(d), me).wait_recv()

    def fwd2(p, q, d):
        c = chunk(node(p, q, -d), p, part_of(d))
        return ag(c, c, p * 20 + 4 + q * 4 + 2 + part_of(d), node(p, 0, d))

    def got_fwd2(p, q, d):
        c = chunk(node(p, q, 2), p, part_of(d))
        ag(c, c, p * 20 + 4 + q * 4 + 2 + part_of(d), me).wait_recv()

    def share(p, a, b, own=False):
        c = chunk(node(p, a, b), p)
        slot = p * 16 + (a % 4) * 4 + b % 4
        src = g_hbm.at[pl.ds(p * 64, 64)] if own else c
        return remote(src, c, sb_s.at[slot], sb_r.at[slot], {"dp": sib})

    def got_share(p, a, b):
        c = chunk(node(p, a, b, other), p)
        slot = p * 16 + (a % 4) * 4 + b % 4
        remote(c, c, sb_s.at[slot], sb_r.at[slot], {"dp": sib}).wait_recv()

    def peer(j):
        return at(j // 8, lax.rem(j // 2, 4)) * 2 + lax.rem(core + lax.rem(j, 2), 2)

    def columns(device):
        return pl.ds(pl.multiple_of(device * width, width), width)

    def x_copy(src_device, dst_device, slot):
        return remote(
            x_hbm.at[:, columns(dst_device)],
            xf.at[pl.ds(pl.multiple_of(src_device * rows, rows), rows)],
            x_s.at[slot], x_r.at[src_device], {"dp": dst_device},
        )

    def a_copy(src_device, dst_device, slot):
        return remote(
            at_hbm.at[:, columns(dst_device)],
            atf.at[pl.ds(pl.multiple_of(src_device * RANK, RANK), RANK)],
            a_s.at[slot], a_r.at[src_device], {"dp": dst_device},
        )

    own_g = pltpu.make_async_copy(g_hbm, g_all.at[pl.ds(pl.multiple_of(me * rows, rows), rows)], loc.at[0])
    own_x = pltpu.make_async_copy(
        x_hbm.at[:, columns(me)], xf.at[pl.ds(pl.multiple_of(me * rows, rows), rows)], loc.at[1]
    )
    own_a = pltpu.make_async_copy(
        at_hbm.at[:, columns(me)], atf.at[pl.ds(pl.multiple_of(me * RANK, RANK), RANK)], loc.at[2]
    )
    dirs = (1, -1)
    for d in dirs:
        for p in range(2):
            first(p, d).start()
    for d in dirs:
        for p in range(2):
            second(p, 0, d).start()
    own_g.start()
    for p in range(2):
        share(p, 0, 0, True).start()

    own_a.start()

    @pl.loop(1, 32)
    def _(j):
        a_copy(me, peer(j), j).start()

    blank = jnp.zeros((16, PAD, 128), BF16)
    upad[:, 0:PAD, :] = blank
    upad[:, PAD + WIN:, :] = blank

    for d in dirs:
        for p in range(2):
            got_first(p, d)
            fwd1(p, d).start()
            for e in dirs:
                second(p, (-d) % 4, e).start()
            share(p, -d, 0).start()
    for d in dirs:
        for p in range(2):
            got_second(p, 0, d)
            fwd2(p, 0, d).start()
            share(p, 0, -d).start()
    for p in range(2):
        for d in dirs:
            got_fwd1(p, d)
        for e in dirs:
            second(p, 2, e).start()
        share(p, 2, 0).start()
    for q in (3, 1):
        for d in dirs:
            for p in range(2):
                got_second(p, q, d)
                fwd2(p, q, d).start()
                share(p, q, -d).start()
    own_x.start()

    @pl.loop(1, 32)
    def _(j):
        x_copy(me, peer(j), j).start()

    for p in range(2):
        for d in dirs:
            got_fwd2(p, 0, d)
        share(p, 0, 2).start()
    for d in dirs:
        for p in range(2):
            got_second(p, 2, d)
            fwd2(p, 2, d).start()
            share(p, 2, -d).start()
    for q in (3, 1, 2):
        for p in range(2):
            for d in dirs:
                got_fwd2(p, q, d)
            share(p, q, 2).start()
    own_g.wait()
    for p in range(2):
        for a in range(4):
            for b in range(4):
                got_share(p, a, b)

    s0 = start_of(me)
    lane = lax.broadcasted_iota(jnp.int32, (WIN, 128), 1)
    ut2 = jnp.concatenate([ut_ref[...], ut_ref[...]], axis=0)
    u_own = (mask[...] * dot(g_all[pl.ds(s0, WIN), :], ut2, NT)).astype(BF16)
    usib[0] = u_own
    to_sib = remote(usib.at[0], usib.at[1], us_s, us_r, {"dp": sib})
    to_sib.start()
    to_sib.wait_recv()
    upad[chip, PAD:PAD + WIN, :] = u_own + usib[1]

    def u_rows(c, part):
        return upad.at[c, pl.ds(pl.multiple_of(PAD + part * HALF, 16), HALF)]

    def u_copy(c, device):
        return remote(u_rows(c, core), u_rows(c, core), u_s.at[device // 2], u_r.at[c], {"dp": device})

    def u_share(c, part):
        return remote(u_rows(c, part), u_rows(c, part), uf_s.at[c], uf_r.at[c], {"dp": sib})

    def chip_at(j):
        return at(j // 4, lax.rem(j, 4))

    @pl.loop(1, 16)
    def _(j):
        u_copy(chip, chip_at(j) * 2 + core).start()

    own_a.wait()

    @pl.loop(1, 32)
    def _(j):
        a_copy(peer(j), me, j).wait_recv()

    @pl.loop(1, 16)
    def _(j):
        c = chip_at(j)
        u_copy(c, c * 2 + core).wait_recv()
        u_share(c, core).start()

    @pl.loop(1, 16)
    def _(j):
        u_share(chip_at(j), other).wait_recv()

    def p_copy(src_device, dst_device):
        return remote(
            p_stage.at[pl.ds(pl.multiple_of(dst_device * rows, rows), rows)],
            passed.at[:, columns(src_device)],
            p_s.at[dst_device], p_r.at[src_device], {"section": lax.rem(z + last, last + 1), "dp": dst_device},
        )

    low = (lax.broadcasted_iota(jnp.int32, (2 * rows, 128), 1) < RANK).astype(F32).astype(BF16)
    high = (lax.broadcasted_iota(jnp.int32, (2 * rows, 128), 1) >= RANK).astype(F32).astype(BF16)

    @pl.when(z > 0)
    def _():
        @pl.loop(0, 16)
        def _(j):
            c = chip_at(j)
            base = pl.multiple_of(c * 2 * rows, 2 * rows)
            for k in range(16):
                even = spots[c * 32 + 2 * k] * 16
                odd = spots[c * 32 + 2 * k + 1] * 16
                uexp[:, k * 128:(k + 1) * 128] = (
                    upad[k, pl.ds(even, 2 * rows), :] * low
                    + upad[k, pl.ds(odd, 2 * rows), :] * high
                )
            tile = dot(g_all[pl.ds(base, 2 * rows), :], w_ref[...], NT)
            tile = tile + 2.0 * dot(uexp[...], atf[...], NN)
            p_stage[pl.ds(base, 2 * rows), :] = tile.astype(BF16)
            p_copy(me, c * 2 + core).start()
            p_copy(me, c * 2 + other).start()

    @pl.when(z == last)
    def _():
        zero[...] = jnp.zeros_like(zero)

        @pl.loop(0, 32)
        def _(j):
            pltpu.make_async_copy(zero, passed.at[:, columns(j)], p_r.at[j]).start()

    own_x.wait()

    @pl.loop(1, 32)
    def _(j):
        x_copy(peer(j), me, j).wait_recv()

    def da_copy(src_device, dst_device):
        return remote(
            da_stage.at[pl.ds(pl.multiple_of(dst_device * RANK, RANK), RANK)],
            da_out.at[:, columns(src_device)],
            da_s.at[dst_device], da_r.at[src_device], {"dp": dst_device},
        )

    own_da = pltpu.make_async_copy(
        da_stage.at[pl.ds(pl.multiple_of(me * RANK, RANK), RANK)], da_out.at[:, columns(me)], loc.at[3]
    )

    @pl.loop(0, 16)
    def _(j):
        c = chip_at(j)
        xe = xf[pl.ds(start_of(2 * c), WIN), :]
        xo = xf[pl.ds(start_of(2 * c + 1), WIN), :]
        pair = atf[pl.ds(pl.multiple_of(c * 128, 128), 128), :]
        vp[c] = jnp.where(lane < RANK, dot(xe, pair, NT), dot(xo, pair, NT))
        u = upad[c, PAD:PAD + WIN, :]
        grad_row = lax.broadcasted_iota(jnp.int32, (128, width), 0)
        da = jnp.where(grad_row < RANK, dot(u, xe, TN), dot(u, xo, TN))
        da_stage[pl.ds(pl.multiple_of(c * 128, 128), 128), :] = (2.0 * da).astype(BF16)

        @pl.when(j == 0)
        def _():
            own_da.start()

        @pl.when(j > 0)
        def _():
            da_copy(me, c * 2 + core).start()

        da_copy(me, c * 2 + other).start()

    def half(part):
        return pl.ds(pl.multiple_of(part * HALF, 8), HALF)

    v_swap = remote(vp.at[:, half(other)], vsib, vs_s, vs_r, {"dp": sib})
    v_swap.start()
    v_swap.wait_recv()

    def v_copy(src_chip, dst_chip):
        return remote(vsib.at[dst_chip], vrecv.at[src_chip], v_s.at[dst_chip], v_r.at[src_chip], {"dp": dst_chip * 2 + core})

    @pl.loop(1, 16)
    def _(j):
        c = chip_at(j)
        vsib[c] = vsib[c] + vp[c, half(core), :]
        v_copy(chip, c).start()

    total = vsib[chip] + vp[chip, half(core), :]

    def add(j, total):
        c = chip_at(j)
        v_copy(c, chip).wait_recv()
        return total + vrecv[c]

    vbf[half_bf(core), :] = lax.fori_loop(1, 16, add, total).astype(BF16)
    v_back = remote(vbf.at[half_bf(core)], vbf.at[half_bf(core)], vb_s, vb_r, {"dp": sib})
    v_back.start()
    remote(vbf.at[half_bf(other)], vbf.at[half_bf(other)], vb_s, vb_r, {"dp": sib}).wait_recv()
    v = (mask[...] * vbf[...].astype(F32)).astype(BF16)

    @pl.loop(0, 4)
    def _(i):
        part = pl.ds(pl.multiple_of(i * 512, 512), 512)
        dubuf[:, part] = (2.0 * dot(v, g_all[pl.ds(s0, WIN), part], TN)).astype(BF16)

    own_du = pltpu.make_async_copy(dubuf.at[pl.ds(pl.multiple_of(core * RANK, RANK), RANK)], du_out, loc.at[4])
    own_du.start()

    own_da.wait()
    own_du.wait()
    to_sib.wait_send()
    v_swap.wait_send()
    v_back.wait_send()
    for p in range(2):
        for d in dirs:
            first(p, d).wait_send()
            fwd1(p, d).wait_send()
            for q in range(4):
                second(p, q, d).wait_send()
                fwd2(p, q, d).wait_send()
        for a in range(4):
            for b in range(4):
                share(p, a, b).wait_send()

    @pl.loop(1, 32)
    def _(j):
        d = peer(j)
        a_copy(me, d, j).wait_send()
        x_copy(me, d, j).wait_send()
        da_copy(me, d).wait_send()
        da_copy(d, me).wait_recv()

    @pl.loop(1, 16)
    def _(j):
        c = chip_at(j)
        u_copy(chip, c * 2 + core).wait_send()
        u_share(c, core).wait_send()
        v_copy(chip, c).wait_send()

    @pl.when(z > 0)
    def _():
        @pl.loop(0, 32)
        def _(j):
            p_copy(me, j).wait_send()

    @pl.when(z < last)
    def _():
        @pl.loop(0, 32)
        def _(j):
            p_copy(j, me).wait_recv()

    @pl.when(z == last)
    def _():
        @pl.loop(0, 32)
        def _(j):
            pltpu.make_async_copy(zero, passed.at[:, columns(j)], p_r.at[j]).wait()


def half_bf(part):
    return pl.ds(pl.multiple_of(part * HALF, 16), HALF)


def local(output_gradient, saved_input, frozen_matrix, down_maps, up_maps, token_tenants, slot_lookup):
    tokens = token_tenants.shape[1]
    tenants = slot_lookup.shape[1]
    order = jnp.arange(tenants, dtype=jnp.int32)
    tenant_of = jnp.sum(jnp.where(slot_lookup[0][None, :] == order[:, None], order[None, :], 0), axis=1)
    row = token_tenants[0][None, :]
    start = jnp.sum((row < tenant_of[:, None]).astype(jnp.int32), axis=1)
    count = jnp.sum((row == tenant_of[:, None]).astype(jnp.int32), axis=1)
    meta = jnp.minimum(start // 16, (tokens - WIN) // 16)
    block = jnp.arange(16, dtype=jnp.int32) * (tokens // 256)
    spots = jnp.clip(PAD // 16 + block[:, None] - meta[None, :], 0, (PAD + WIN) // 16).reshape(-1)
    me = lax.axis_index("dp")
    place = jnp.arange(WIN, dtype=jnp.int32)[:, None]
    begin, size, first = (jnp.sum(jnp.where(order == me, t, 0)) for t in (start, count, meta * 16))
    side = jnp.arange(128, dtype=jnp.int32)[None, :] // RANK
    live = (place >= begin - first) & (place < begin - first + size) & (side == me % 2)
    mask = live.astype(F32)

    rows, kv = output_gradient.shape[1:]
    model = saved_input.shape[2]
    width = frozen_matrix.shape[1]
    hbm = pl.BlockSpec(memory_space=pl.ANY)
    vmem = pl.BlockSpec(memory_space=pltpu.VMEM)
    smem = pl.BlockSpec(memory_space=pltpu.SMEM)
    dma = pltpu.SemaphoreType.DMA
    passed, da, du = pl.pallas_call(
        kernel,
        out_shape=(
            jax.ShapeDtypeStruct((rows, model), BF16),
            jax.ShapeDtypeStruct((RANK, model), BF16),
            jax.ShapeDtypeStruct((RANK, kv), BF16),
        ),
        in_specs=[smem, smem, vmem, hbm, hbm, vmem, hbm, vmem],
        out_specs=(hbm, hbm, hbm),
        scratch_shapes=[
            pltpu.VMEM((tokens, kv), BF16),
            pltpu.VMEM((tokens, width), BF16),
            pltpu.VMEM((tenants * RANK, width), BF16),
            pltpu.VMEM((16, PAD + WIN + PAD, 128), BF16),
            pltpu.VMEM((2, WIN, 128), BF16),
            pltpu.VMEM((2 * rows, tenants * RANK), BF16),
            pltpu.VMEM((tokens, width), BF16),
            pltpu.VMEM((tenants * RANK, width), BF16),
            pltpu.VMEM((16, WIN, 128), F32),
            pltpu.VMEM((16, HALF, 128), F32),
            pltpu.VMEM((16, HALF, 128), F32),
            pltpu.VMEM((WIN, 128), BF16),
            pltpu.VMEM((128, kv), BF16),
            pltpu.VMEM((rows, width), BF16),
            dma((5,)),
            dma((40,)), dma((40,)), dma((32,)), dma((32,)),
            dma((32,)), dma((32,)), dma((32,)), dma((32,)),
            dma, dma, dma((16,)), dma((16,)), dma((16,)), dma((16,)),
            dma((32,)), dma((32,)), dma((32,)), dma((32,)),
            dma, dma, dma((16,)), dma((16,)), dma, dma,
        ],
        compiler_params=pltpu.CompilerParams(has_side_effects=True, vmem_limit_bytes=56 << 20),
    )(
        meta,
        spots,
        mask,
        output_gradient[0],
        saved_input[0],
        frozen_matrix[0],
        jnp.swapaxes(down_maps[0], 0, 1),
        jnp.swapaxes(up_maps[0], 0, 1),
    )
    return passed[None], jnp.swapaxes(da, 0, 1)[None], jnp.swapaxes(du, 0, 1)[None]


def solution(mesh):
    return jax.shard_map(
        local,
        mesh=mesh,
        in_specs=(
            P("section", "dp", None),
            P("section", "dp", None),
            P("section", "dp", None),
            P("section", None, "dp"),
            P("section", None, "dp"),
            P("section", None),
            P("section", None),
        ),
        out_specs=(P("section", "dp", None), P("section", None, "dp"), P("section", None, "dp")),
        check_vma=False,
    )
```

time: 440 us -> 209 us (0.47)
  the two profiles are of different devices: /device:TPU:1 before, /device:TPU:33 now
where the time goes in v1:
time: 209 us
  Pallas kernels  198 us (95%)
  local copies, waits for them, and re-layouts  5.54 us (3%)
  other arithmetic  3.31 us (2%)
  between operations  2.64 us (1%)
    pallas_call x1, Pallas kernels, local(): pl.pallas_call(kernel, out_shape=(jax.ShapeDtypeStruct((rows, model), BF1...  198 us
    unnamed x9, local copies, waits for them, and re-layouts  4.88 us

profile of v1, /device:TPU:33, one launch (start us, length us, event | category | flops | bytes accessed | tf_op | source)
XLA Modules:
  0.0 209.2 jit_solution(16439922799985102237)
XLA Ops:
  0.7 0.8 select_reduce_fusion
  1.4 1.0 convert_reduce_fusion
  2.4 0.7 select_reduce_fusion.2
  3.1 0.0 copy-start.2
  5.1 0.1 subtract_clamp_fusion
  5.2 0.7 min.20.spots
  5.8 0.8 and_convert_fusion.mask
  6.6 0.0 copy-done.2
  6.6 197.7 %shard_map.94 = (bf16[128,8192]{1,0:T(8,128)(2,1)}, bf16[64,8192]{1,0:T(8,128)(2,1)}, bf16[64,2048]{1,0:T(8,128)(2,1)}) custom-call(s32[32]{0:T(128)} %copy-done.2, s32[512]{0:T(512)} %min.20.spots, f32[288,128]{1,0:T(8,128)} %and_convert_fusion.mask, bf16[128,2048]{1,0:T(8,128)(2,1)} %bitcast.23, bf16[128,8192]{1,0:T(8,128)(2,1)} %bitcast.18, ...), custom_call_target="tpu_custom_call" | custom-call | tf_op jit(solution)/shard_map/pallas_call | solution.py:443
  204.3 0.0 copy-start
  204.3 0.0 copy-start.1
  204.3 3.2 %copy.13 = bf16[1,128,8192]{2,1,0:T(8,128)(2,1)} copy(bf16[1,128,8192]{2,1,0:T(8,128)(2,1)} %bitcast.19) | data formatting | bytes 4194304
  207.5 0.0 copy-done
  207.5 1.0 copy.14
  208.5 0.0 copy-done.1
  208.5 0.7 copy.15
  (3 shorter events, 0.0 us)
Async XLA Ops:
  3.1 3.5 %copy-start.2 = (s32[32]{0:T(128)}, s32[32]{0:T(128)S(1)}, u32[]{:S(2)}) copy-start(s32[32]{0:T(128)S(1)} %get-tuple-element.12.meta) | copy-start | bytes 388
  204.3 3.2 %copy-start = (bf16[64,8192]{1,0:T(8,128)(2,1)S(1)}, bf16[64,8192]{1,0:T(8,128)(2,1)}, u32[]{:S(2)}) copy-start(bf16[64,8192]{1,0:T(8,128)(2,1)} %get-tuple-element.7) | copy-start | bytes 3145732
  204.3 4.2 %copy-start.1 = (bf16[64,2048]{1,0:T(8,128)(2,1)S(1)}, bf16[64,2048]{1,0:T(8,128)(2,1)}, u32[]{:S(2)}) copy-start(bf16[64,2048]{1,0:T(8,128)(2,1)} %get-tuple-element.8) | copy-start | bytes 786436

commit v2 on v1

--- a/solution.py
+++ b/solution.py
@@ -30,7 +30,7 @@
 def kernel(
     meta, spots, mask, g_hbm, x_hbm, w_ref, at_hbm, ut_ref, passed, da_out, du_out,
     g_all, xf, atf, upad, usib, uexp, p_stage, da_stage, vp, vsib, vrecv, vbf, dubuf, zero,
-    loc, ag_s, ag_r, sb_s, sb_r, x_s, x_r, a_s, a_r, us_s, us_r, u_s, u_r, uf_s, uf_r,
+    ready, loc, ag_s, ag_r, sb_s, sb_r, x_s, x_r, a_s, a_r, us_s, us_r, u_s, u_r, uf_s, uf_r,
     p_s, p_r, da_s, da_r, vs_s, vs_r, v_s, v_r, vb_s, vb_r,
 ):
     z = lax.axis_index("section")
@@ -50,6 +50,18 @@
     def start_of(slot):
         return meta[slot] * 16
 
+    sections = last + 1
+    barrier = pltpu.get_barrier_semaphore()
+
+    @pl.loop(1, 32)
+    def _(j):
+        pl.semaphore_signal(barrier, 1, device_id={"dp": lax.rem(me + j, 32)}, device_id_type=MESH)
+
+    for step in (1, last):
+        pl.semaphore_signal(barrier, 1, device_id={"section": lax.rem(z + step, sections)}, device_id_type=MESH)
+    pl.semaphore_wait(barrier, 33)
+    pl.semaphore_signal(ready, 1, device_id={"section": lax.rem(z + 1, sections)}, device_id_type=MESH)
+
     def node(p, a, b, who=core):
         return (at(b % 4, a % 4) if p == 0 else at(a % 4, b % 4)) * 2 + who
 
@@ -108,8 +120,11 @@
         slot = p * 16 + (a % 4) * 4 + b % 4
         remote(c, c, sb_s.at[slot], sb_r.at[slot], {"dp": sib}).wait_recv()
 
+    def chip_at(j):
+        return at(lax.rem(j, 4), lax.rem(j + j // 4, 4))
+
     def peer(j):
-        return at(j // 8, lax.rem(j // 2, 4)) * 2 + lax.rem(core + lax.rem(j, 2), 2)
+        return chip_at(j // 2) * 2 + lax.rem(core + lax.rem(j, 2), 2)
 
     def columns(device):
         return pl.ds(pl.multiple_of(device * width, width), width)
@@ -225,9 +240,6 @@
     def u_share(c, part):
         return remote(u_rows(c, part), u_rows(c, part), uf_s.at[c], uf_r.at[c], {"dp": sib})
 
-    def chip_at(j):
-        return at(j // 4, lax.rem(j, 4))
-
     @pl.loop(1, 16)
     def _(j):
         u_copy(chip, chip_at(j) * 2 + core).start()
@@ -237,6 +249,25 @@
     @pl.loop(1, 32)
     def _(j):
         a_copy(peer(j), me, j).wait_recv()
+
+    own_x.wait()
+
+    @pl.loop(1, 32)
+    def _(j):
+        x_copy(peer(j), me, j).wait_recv()
+
+    @pl.loop(0, 16)
+    def _(c):
+        pair = atf[pl.ds(pl.multiple_of(c * 128, 128), 128), :]
+        even = dot(xf[pl.ds(start_of(2 * c), WIN), :], pair, NT)
+        odd = dot(xf[pl.ds(start_of(2 * c + 1), WIN), :], pair, NT)
+        vp[c] = jnp.where(lane < RANK, even, odd)
+
+    def half(part):
+        return pl.ds(pl.multiple_of(part * HALF, 8), HALF)
+
+    v_swap = remote(vp.at[:, half(other)], vsib, vs_s, vs_r, {"dp": sib})
+    v_swap.start()
 
     @pl.loop(1, 16)
     def _(j):
@@ -244,9 +275,22 @@
         u_copy(c, c * 2 + core).wait_recv()
         u_share(c, core).start()
 
+    def v_copy(src_chip, dst_chip):
+        return remote(vsib.at[dst_chip], vrecv.at[src_chip], v_s.at[dst_chip], v_r.at[src_chip], {"dp": dst_chip * 2 + core})
+
+    v_swap.wait_recv()
+
     @pl.loop(1, 16)
     def _(j):
+        c = chip_at(j)
+        vsib[c] = vsib[c] + vp[c, half(core), :]
+        v_copy(chip, c).start()
+
+    @pl.loop(1, 16)
+    def _(j):
         u_share(chip_at(j), other).wait_recv()
+
+    pl.semaphore_wait(ready, 1)
 
     def p_copy(src_device, dst_device):
         return remote(
@@ -258,18 +302,29 @@
     low = (lax.broadcasted_iota(jnp.int32, (2 * rows, 128), 1) < RANK).astype(F32).astype(BF16)
     high = (lax.broadcasted_iota(jnp.int32, (2 * rows, 128), 1) >= RANK).astype(F32).astype(BF16)
 
-    @pl.when(z > 0)
-    def _():
-        @pl.loop(0, 16)
-        def _(j):
-            c = chip_at(j)
+    def da_copy(src_device, dst_device):
+        return remote(
+            da_stage.at[pl.ds(pl.multiple_of(dst_device * RANK, RANK), RANK)],
+            da_out.at[:, columns(src_device)],
+            da_s.at[dst_device], da_r.at[src_device], {"dp": dst_device},
+        )
+
+    own_da = pltpu.make_async_copy(
+        da_stage.at[pl.ds(pl.multiple_of(me * RANK, RANK), RANK)], da_out.at[:, columns(me)], loc.at[3]
+    )
+
+    @pl.loop(0, 16)
+    def _(j):
+        c = chip_at(j)
+
+        @pl.when(z > 0)
+        def _():
             base = pl.multiple_of(c * 2 * rows, 2 * rows)
             for k in range(16):
                 even = spots[c * 32 + 2 * k] * 16
                 odd = spots[c * 32 + 2 * k + 1] * 16
                 uexp[:, k * 128:(k + 1) * 128] = (
-                    upad[k, pl.ds(even, 2 * rows), :] * low
-                    + upad[k, pl.ds(odd, 2 * rows), :] * high
+                    upad[k, pl.ds(even, 2 * rows), :] * low + upad[k, pl.ds(odd, 2 * rows), :] * high
                 )
             tile = dot(g_all[pl.ds(base, 2 * rows), :], w_ref[...], NT)
             tile = tile + 2.0 * dot(uexp[...], atf[...], NN)
@@ -277,6 +332,24 @@
             p_copy(me, c * 2 + core).start()
             p_copy(me, c * 2 + other).start()
 
+        u = upad[c, PAD:PAD + WIN, :]
+        even = dot(u, xf[pl.ds(start_of(2 * c), WIN), :], TN)
+        odd = dot(u, xf[pl.ds(start_of(2 * c + 1), WIN), :], TN)
+        grad_row = lax.broadcasted_iota(jnp.int32, (128, width), 0)
+        da_stage[pl.ds(pl.multiple_of(c * 128, 128), 128), :] = (
+            2.0 * jnp.where(grad_row < RANK, even, odd)
+        ).astype(BF16)
+
+        @pl.when(j == 0)
+        def _():
+            own_da.start()
+
+        @pl.when(j > 0)
+        def _():
+            da_copy(me, c * 2 + core).start()
+
+        da_copy(me, c * 2 + other).start()
+
     @pl.when(z == last)
     def _():
         zero[...] = jnp.zeros_like(zero)
@@ -284,61 +357,6 @@
         @pl.loop(0, 32)
         def _(j):
             pltpu.make_async_copy(zero, passed.at[:, columns(j)], p_r.at[j]).start()
-
-    own_x.wait()
-
-    @pl.loop(1, 32)
-    def _(j):
-        x_copy(peer(j), me, j).wait_recv()
-
-    def da_copy(src_device, dst_device):
-        return remote(
-            da_stage.at[pl.ds(pl.multiple_of(dst_device * RANK, RANK), RANK)],
-            da_out.at[:, columns(src_device)],
-            da_s.at[dst_device], da_r.at[src_device], {"dp": dst_device},
-        )
-
-    own_da = pltpu.make_async_copy(
-        da_stage.at[pl.ds(pl.multiple_of(me * RANK, RANK), RANK)], da_out.at[:, columns(me)], loc.at[3]
-    )
-
-    @pl.loop(0, 16)
-    def _(j):
-        c = chip_at(j)
-        xe = xf[pl.ds(start_of(2 * c), WIN), :]
-        xo = xf[pl.ds(start_of(2 * c + 1), WIN), :]
-        pair = atf[pl.ds(pl.multiple_of(c * 128, 128), 128), :]
-        vp[c] = jnp.where(lane < RANK, dot(xe, pair, NT), dot(xo, pair, NT))
-        u = upad[c, PAD:PAD + WIN, :]
-        grad_row = lax.broadcasted_iota(jnp.int32, (128, width), 0)
-        da = jnp.where(grad_row < RANK, dot(u, xe, TN), dot(u, xo, TN))
-        da_stage[pl.ds(pl.multiple_of(c * 128, 128), 128), :] = (2.0 * da).astype(BF16)
-
-        @pl.when(j == 0)
-        def _():
-            own_da.start()
-
-        @pl.when(j > 0)
-        def _():
-            da_copy(me, c * 2 + core).start()
-
-        da_copy(me, c * 2 + other).start()
-
-    def half(part):
-        return pl.ds(pl.multiple_of(part * HALF, 8), HALF)
-
-    v_swap = remote(vp.at[:, half(other)], vsib, vs_s, vs_r, {"dp": sib})
-    v_swap.start()
-    v_swap.wait_recv()
-
-    def v_copy(src_chip, dst_chip):
-        return remote(vsib.at[dst_chip], vrecv.at[src_chip], v_s.at[dst_chip], v_r.at[src_chip], {"dp": dst_chip * 2 + core})
-
-    @pl.loop(1, 16)
-    def _(j):
-        c = chip_at(j)
-        vsib[c] = vsib[c] + vp[c, half(core), :]
-        v_copy(chip, c).start()
 
     total = vsib[chip] + vp[chip, half(core), :]
 
@@ -464,6 +482,7 @@
             pltpu.VMEM((WIN, 128), BF16),
             pltpu.VMEM((128, kv), BF16),
             pltpu.VMEM((rows, width), BF16),
+            pltpu.SemaphoreType.REGULAR,
             dma((5,)),
             dma((40,)), dma((40,)), dma((32,)), dma((32,)),
             dma((32,)), dma((32,)), dma((32,)), dma((32,)),
@@ -471,7 +490,7 @@
             dma((32,)), dma((32,)), dma((32,)), dma((32,)),
             dma, dma, dma((16,)), dma((16,)), dma, dma,
         ],
-        compiler_params=pltpu.CompilerParams(has_side_effects=True, vmem_limit_bytes=56 << 20),
+        compiler_params=pltpu.CompilerParams(collective_id=0, has_side_effects=True, vmem_limit_bytes=56 << 20),
     )(
         meta,
         spots,

time: 209 us -> 179 us (0.86)
  the two profiles are of different devices: /device:TPU:33 before, /device:TPU:1 now
where the time goes in v2:
time: 179 us
  Pallas kernels  168 us (94%)
  local copies, waits for them, and re-layouts  5.54 us (3%)
  other arithmetic  3.31 us (2%)
  between operations  2.64 us (1%)
    pallas_call x1, Pallas kernels, local(): pl.pallas_call(kernel, out_shape=(jax.ShapeDtypeStruct((rows, model), BF1...  168 us
    unnamed x9, local copies, waits for them, and re-layouts  4.88 us

profile of v2, /device:TPU:1, one launch (start us, length us, event | category | flops | bytes accessed | tf_op | source)
XLA Modules:
  0.0 179.0 jit_solution(9385338300789421822)
XLA Ops:
  0.7 0.8 select_reduce_fusion
  1.4 1.0 convert_reduce_fusion
  2.4 0.7 select_reduce_fusion.2
  3.1 0.0 copy-start.2
  5.1 0.1 subtract_clamp_fusion
  5.2 0.7 min.20.spots
  5.8 0.8 and_convert_fusion.mask
  6.6 0.0 copy-done.2
  6.6 167.5 %shard_map.94 = (bf16[128,8192]{1,0:T(8,128)(2,1)}, bf16[64,8192]{1,0:T(8,128)(2,1)}, bf16[64,2048]{1,0:T(8,128)(2,1)}) custom-call(s32[32]{0:T(128)} %copy-done.2, s32[512]{0:T(512)} %min.20.spots, f32[288,128]{1,0:T(8,128)} %and_convert_fusion.mask, bf16[128,2048]{1,0:T(8,128)(2,1)} %bitcast.23, bf16[128,8192]{1,0:T(8,128)(2,1)} %bitcast.18, ...), custom_call_target="tpu_custom_call" | custom-call | tf_op jit(solution)/shard_map/pallas_call | solution.py:461
  174.1 0.0 copy-start
  174.1 0.0 copy-start.1
  174.1 3.2 %copy.13 = bf16[1,128,8192]{2,1,0:T(8,128)(2,1)} copy(bf16[1,128,8192]{2,1,0:T(8,128)(2,1)} %bitcast.19) | data formatting | bytes 4194304
  177.3 0.0 copy-done
  177.3 1.0 copy.14
  178.3 0.0 copy-done.1
  178.3 0.7 copy.15
  (3 shorter events, 0.0 us)
Async XLA Ops:
  3.1 3.5 %copy-start.2 = (s32[32]{0:T(128)}, s32[32]{0:T(128)S(1)}, u32[]{:S(2)}) copy-start(s32[32]{0:T(128)S(1)} %get-tuple-element.12.meta) | copy-start | bytes 388
  174.1 3.2 %copy-start = (bf16[64,8192]{1,0:T(8,128)(2,1)S(1)}, bf16[64,8192]{1,0:T(8,128)(2,1)}, u32[]{:S(2)}) copy-start(bf16[64,8192]{1,0:T(8,128)(2,1)} %get-tuple-element.7) | copy-start | bytes 3145732
  174.1 4.2 %copy-start.1 = (bf16[64,2048]{1,0:T(8,128)(2,1)S(1)}, bf16[64,2048]{1,0:T(8,128)(2,1)}, u32[]{:S(2)}) copy-start(bf16[64,2048]{1,0:T(8,128)(2,1)} %get-tuple-element.8) | copy-start | bytes 786436

commit v3 on v2

--- a/solution.py
+++ b/solution.py
@@ -36,34 +36,34 @@
     z = lax.axis_index("section")
     me = lax.axis_index("dp")
     last = lax.axis_size("section") - 1
-    core = lax.rem(me, 2)
-    other = 1 - core
-    chip = me // 2
-    x, y = chip // 4, lax.rem(chip, 4)
-    sib = chip * 2 + other
+    core = me & 1
+    other = core ^ 1
+    chip = me >> 1
+    sib = me ^ 1
+    along_x = [((me >> 3) + d & 3) * 8 for d in range(4)]
+    along_y = [(chip + d & 3) * 2 for d in range(4)]
+    after = jnp.where(z == last, 0, z + 1)
+    before = jnp.where(z == 0, last, z - 1)
     width = w_ref.shape[0]
     rows = g_hbm.shape[0]
 
-    def at(dx, dy):
-        return lax.rem(x + dx, 4) * 4 + lax.rem(y + dy, 4)
-
     def start_of(slot):
         return meta[slot] * 16
 
-    sections = last + 1
     barrier = pltpu.get_barrier_semaphore()
 
     @pl.loop(1, 32)
     def _(j):
-        pl.semaphore_signal(barrier, 1, device_id={"dp": lax.rem(me + j, 32)}, device_id_type=MESH)
-
-    for step in (1, last):
-        pl.semaphore_signal(barrier, 1, device_id={"section": lax.rem(z + step, sections)}, device_id_type=MESH)
+        pl.semaphore_signal(barrier, 1, device_id={"dp": me ^ j}, device_id_type=MESH)
+
+    for section in (after, before):
+        pl.semaphore_signal(barrier, 1, device_id={"section": section}, device_id_type=MESH)
     pl.semaphore_wait(barrier, 33)
-    pl.semaphore_signal(ready, 1, device_id={"section": lax.rem(z + 1, sections)}, device_id_type=MESH)
+    pl.semaphore_signal(ready, 1, device_id={"section": after}, device_id_type=MESH)
 
     def node(p, a, b, who=core):
-        return (at(b % 4, a % 4) if p == 0 else at(a % 4, b % 4)) * 2 + who
+        dx, dy = (b, a) if p == 0 else (a, b)
+        return along_x[dx % 4] + along_y[dy % 4] + who
 
     def chunk(device, p, part=None):
         first = device * rows + p * 64
@@ -121,10 +121,10 @@
         remote(c, c, sb_s.at[slot], sb_r.at[slot], {"dp": sib}).wait_recv()
 
     def chip_at(j):
-        return at(lax.rem(j, 4), lax.rem(j + j // 4, 4))
+        return chip ^ (j * 5 & 15)
 
     def peer(j):
-        return chip_at(j // 2) * 2 + lax.rem(core + lax.rem(j, 2), 2)
+        return me ^ (((j >> 1) * 5 & 15) * 2 + (j & 1))
 
     def columns(device):
         return pl.ds(pl.multiple_of(device * width, width), width)
@@ -195,12 +195,6 @@
                 got_second(p, q, d)
                 fwd2(p, q, d).start()
                 share(p, q, -d).start()
-    own_x.start()
-
-    @pl.loop(1, 32)
-    def _(j):
-        x_copy(me, peer(j), j).start()
-
     for p in range(2):
         for d in dirs:
             got_fwd2(p, 0, d)
@@ -215,6 +209,12 @@
             for d in dirs:
                 got_fwd2(p, q, d)
             share(p, q, 2).start()
+    own_x.start()
+
+    @pl.loop(1, 32)
+    def _(j):
+        x_copy(me, peer(j), j).start()
+
     own_g.wait()
     for p in range(2):
         for a in range(4):
@@ -235,7 +235,7 @@
         return upad.at[c, pl.ds(pl.multiple_of(PAD + part * HALF, 16), HALF)]
 
     def u_copy(c, device):
-        return remote(u_rows(c, core), u_rows(c, core), u_s.at[device // 2], u_r.at[c], {"dp": device})
+        return remote(u_rows(c, core), u_rows(c, core), u_s.at[device >> 1], u_r.at[c], {"dp": device})
 
     def u_share(c, part):
         return remote(u_rows(c, part), u_rows(c, part), uf_s.at[c], uf_r.at[c], {"dp": sib})
@@ -296,7 +296,7 @@
         return remote(
             p_stage.at[pl.ds(pl.multiple_of(dst_device * rows, rows), rows)],
             passed.at[:, columns(src_device)],
-            p_s.at[dst_device], p_r.at[src_device], {"section": lax.rem(z + last, last + 1), "dp": dst_device},
+            p_s.at[dst_device], p_r.at[src_device], {"section": before, "dp": dst_device},
         )
 
     low = (lax.broadcasted_iota(jnp.int32, (2 * rows, 128), 1) < RANK).astype(F32).astype(BF16)
@@ -321,8 +321,8 @@
         def _():
             base = pl.multiple_of(c * 2 * rows, 2 * rows)
             for k in range(16):
-                even = spots[c * 32 + 2 * k] * 16
-                odd = spots[c * 32 + 2 * k + 1] * 16
+                even = spots[c, 2 * k] * 16
+                odd = spots[c, 2 * k + 1] * 16
                 uexp[:, k * 128:(k + 1) * 128] = (
                     upad[k, pl.ds(even, 2 * rows), :] * low + upad[k, pl.ds(odd, 2 * rows), :] * high
                 )
@@ -443,13 +443,13 @@
     count = jnp.sum((row == tenant_of[:, None]).astype(jnp.int32), axis=1)
     meta = jnp.minimum(start // 16, (tokens - WIN) // 16)
     block = jnp.arange(16, dtype=jnp.int32) * (tokens // 256)
-    spots = jnp.clip(PAD // 16 + block[:, None] - meta[None, :], 0, (PAD + WIN) // 16).reshape(-1)
+    spots = jnp.clip(PAD // 16 + block[:, None] - meta[None, :], 0, (PAD + WIN) // 16)
     me = lax.axis_index("dp")
     place = jnp.arange(WIN, dtype=jnp.int32)[:, None]
-    begin, size, first = (jnp.sum(jnp.where(order == me, t, 0)) for t in (start, count, meta * 16))
-    side = jnp.arange(128, dtype=jnp.int32)[None, :] // RANK
-    live = (place >= begin - first) & (place < begin - first + size) & (side == me % 2)
-    mask = live.astype(F32)
+    offset = (start - meta * 16)[None, :]
+    live = (place >= offset) & (place < offset + count[None, :]) & (order == me)[None, :]
+    side = jnp.arange(128, dtype=jnp.int32)[None, :] >> 6
+    mask = jnp.sum(live.astype(F32), axis=1, keepdims=True) * (side == (me & 1)).astype(F32)
 
     rows, kv = output_gradient.shape[1:]
     model = saved_input.shape[2]

time: 179 us -> 169 us (0.944)
  Pallas kernels: 168 us -> 160 us
  between operations: 2.64 us -> 0.7 us
    pallas_call x1, Pallas kernels: 168 us -> 160 us  [local(): pl.pallas_call(kernel, out_shape=(jax.ShapeDtypeStruct((rows, model), BF1...]
where the time goes in v3:
time: 169 us
  Pallas kernels  160 us (95%)
  local copies, waits for them, and re-layouts  4.88 us (3%)
  other arithmetic  3.33 us (2%)
    pallas_call x1, Pallas kernels, local(): pl.pallas_call(kernel, out_shape=(jax.ShapeDtypeStruct((rows, model), BF1...  160 us
    unnamed x9, local copies, waits for them, and re-layouts  4.88 us

profile of v3, /device:TPU:1, one launch (start us, length us, event | category | flops | bytes accessed | tf_op | source)
XLA Modules:
  0.0 169.1 jit_solution(17168535962646791454)
XLA Ops:
  0.7 0.8 select_reduce_fusion
  1.4 1.0 convert_reduce_fusion
  2.5 0.0 copy-start.2
  2.5 0.1 convert_reduce_fusion.2
  2.6 0.7 subtract_clamp_fusion.spots
  3.2 0.8 broadcast_multiply_fusion.mask
  4.0 0.0 copy-done.2
  4.0 160.2 %shard_map.94 = (bf16[128,8192]{1,0:T(8,128)(2,1)}, bf16[64,8192]{1,0:T(8,128)(2,1)}, bf16[64,2048]{1,0:T(8,128)(2,1)}) custom-call(s32[32]{0:T(128)} %copy-done.2, s32[16,32]{1,0:T(8,128)} %subtract_clamp_fusion.spots, f32[288,128]{1,0:T(8,128)} %broadcast_multiply_fusion.mask, bf16[128,2048]{1,0:T(8,128)(2,1)} %bitcast.23, bf16[128,8192]{1,0:T(8,128)(2,1)} %bitcast.18, ...), custom_call_target="tpu_custom_call" | custom-call | tf_op jit(solution)/shard_map/pallas_call | solution.py:461
  164.2 0.0 copy-start
  164.2 0.0 copy-start.1
  164.2 3.2 %copy.13 = bf16[1,128,8192]{2,1,0:T(8,128)(2,1)} copy(bf16[1,128,8192]{2,1,0:T(8,128)(2,1)} %bitcast.19) | data formatting | bytes 4194304
  167.4 0.0 copy-done
  167.4 1.0 copy.14
  168.4 0.0 copy-done.1
  168.4 0.7 copy.15
  (4 shorter events, 0.0 us)
Async XLA Ops:
  2.5 1.6 copy-start.2
  164.2 3.2 %copy-start = (bf16[64,8192]{1,0:T(8,128)(2,1)S(1)}, bf16[64,8192]{1,0:T(8,128)(2,1)}, u32[]{:S(2)}) copy-start(bf16[64,8192]{1,0:T(8,128)(2,1)} %get-tuple-element.7) | copy-start | bytes 3145732
  164.2 4.2 %copy-start.1 = (bf16[64,2048]{1,0:T(8,128)(2,1)S(1)}, bf16[64,2048]{1,0:T(8,128)(2,1)}, u32[]{:S(2)}) copy-start(bf16[64,2048]{1,0:T(8,128)(2,1)} %get-tuple-element.8) | copy-start | bytes 786436

commit v4 on v3

--- a/solution.py
+++ b/solution.py
@@ -124,7 +124,7 @@
         return chip ^ (j * 5 & 15)
 
     def peer(j):
-        return me ^ (((j >> 1) * 5 & 15) * 2 + (j & 1))
+        return me ^ ((j * 5 & 15) * 2 + (j >> 4))
 
     def columns(device):
         return pl.ds(pl.multiple_of(device * width, width), width)
@@ -162,10 +162,6 @@
         share(p, 0, 0, True).start()
 
     own_a.start()
-
-    @pl.loop(1, 32)
-    def _(j):
-        a_copy(me, peer(j), j).start()
 
     blank = jnp.zeros((16, PAD, 128), BF16)
     upad[:, 0:PAD, :] = blank
@@ -209,6 +205,10 @@
             for d in dirs:
                 got_fwd2(p, q, d)
             share(p, q, 2).start()
+    @pl.loop(1, 32)
+    def _(j):
+        a_copy(me, peer(j), j).start()
+
     own_x.start()
 
     @pl.loop(1, 32)
@@ -332,6 +332,9 @@
             p_copy(me, c * 2 + core).start()
             p_copy(me, c * 2 + other).start()
 
+    @pl.loop(0, 16)
+    def _(j):
+        c = chip_at(j)
         u = upad[c, PAD:PAD + WIN, :]
         even = dot(u, xf[pl.ds(start_of(2 * c), WIN), :], TN)
         odd = dot(u, xf[pl.ds(start_of(2 * c + 1), WIN), :], TN)

time: 169 us -> 166 us (0.982)
  Pallas kernels: 160 us -> 157 us
    pallas_call x1, Pallas kernels: 160 us -> 157 us  [local(): pl.pallas_call(kernel, out_shape=(jax.ShapeDtypeStruct((rows, model), BF1...]
where the time goes in v4:
time: 166 us
  Pallas kernels  157 us (95%)
  local copies, waits for them, and re-layouts  4.88 us (3%)
  other arithmetic  3.33 us (2%)
    pallas_call x1, Pallas kernels, local(): pl.pallas_call(kernel, out_shape=(jax.ShapeDtypeStruct((rows, model), BF1...  157 us
    unnamed x9, local copies, waits for them, and re-layouts  4.88 us

profile of v4, /device:TPU:1, one launch (start us, length us, event | category | flops | bytes accessed | tf_op | source)
XLA Modules:
  0.0 166.2 jit_solution(11071201736538299762)
XLA Ops:
  0.7 0.8 select_reduce_fusion
  1.4 1.0 convert_reduce_fusion
  2.5 0.0 copy-start.2
  2.5 0.1 convert_reduce_fusion.2
  2.6 0.7 subtract_clamp_fusion.spots
  3.2 0.8 broadcast_multiply_fusion.mask
  4.0 0.0 copy-done.2
  4.0 157.3 %shard_map.94 = (bf16[128,8192]{1,0:T(8,128)(2,1)}, bf16[64,8192]{1,0:T(8,128)(2,1)}, bf16[64,2048]{1,0:T(8,128)(2,1)}) custom-call(s32[32]{0:T(128)} %copy-done.2, s32[16,32]{1,0:T(8,128)} %subtract_clamp_fusion.spots, f32[288,128]{1,0:T(8,128)} %broadcast_multiply_fusion.mask, bf16[128,2048]{1,0:T(8,128)(2,1)} %bitcast.23, bf16[128,8192]{1,0:T(8,128)(2,1)} %bitcast.18, ...), custom_call_target="tpu_custom_call" | custom-call | tf_op jit(solution)/shard_map/pallas_call | solution.py:464
  161.3 0.0 copy-start
  161.3 0.0 copy-start.1
  161.3 3.2 %copy.13 = bf16[1,128,8192]{2,1,0:T(8,128)(2,1)} copy(bf16[1,128,8192]{2,1,0:T(8,128)(2,1)} %bitcast.19) | data formatting | bytes 4194304
  164.5 0.0 copy-done
  164.5 1.0 copy.14
  165.5 0.0 copy-done.1
  165.5 0.7 copy.15
  (4 shorter events, 0.0 us)
Async XLA Ops:
  2.5 1.6 copy-start.2
  161.3 3.2 %copy-start = (bf16[64,8192]{1,0:T(8,128)(2,1)S(1)}, bf16[64,8192]{1,0:T(8,128)(2,1)}, u32[]{:S(2)}) copy-start(bf16[64,8192]{1,0:T(8,128)(2,1)} %get-tuple-element.7) | copy-start | bytes 3145732
  161.3 4.2 %copy-start.1 = (bf16[64,2048]{1,0:T(8,128)(2,1)S(1)}, bf16[64,2048]{1,0:T(8,128)(2,1)}, u32[]{:S(2)}) copy-start(bf16[64,2048]{1,0:T(8,128)(2,1)} %get-tuple-element.8) | copy-start | bytes 786436
